TPU v7x, 256 devices: a whole 4x4x8 slice. The times are simulated.
256 devices in a mesh: expert: 32 (over y, x, core), group: 8 (over z).
Axes of the slice: x: 4, y: 4, z: 8, core: 2. Of those that a mesh axis runs over, the one named last changes fastest.
Arguments:
- activations: bfloat16 [4096, 7168], P('expert', 'group'), may hold values from -6 to 6
- out_grads: bfloat16 [4096, 7168], P('expert', 'group'), may hold values from -6 to 6
- sketch_op: bfloat16 [7168, 128], P('group'), may hold values from -0.0625 to 0.0625
- block_lists: int32 [256, 32], P('expert'), may hold values from 0 to 31, as said below
- block_counts: int32 [256], P('expert'), may hold values from 1 to 32
- gate_values: bfloat16 [256, 32, 128], P('expert'), may hold values from 0.05 to 9, as said below
Outputs:
- basis_out: float32 [256, 7168, 128], P('expert', 'group')
Inputs may be any that keep to these rules, and one draw needn't show every extreme that they name: `block_lists`: each row is an ordering of all 32 block numbers, each once. `gate_values`: positive.
All inputs are finite; a program needn't handle non-finite values.
Results may differ from a plain program's by a relative error of at most 0.0042.
The roundings to bfloat16 on the way count: a program that leaves them out, or rounds other values in their place, can miss the bound.
Values may be sent and summed in bfloat16 or wider, within the bound.
No kernel may reach another device: no remote copies, remote signals or barrier semaphores. Data moves between devices by JAX's collectives and lax.ppermute only.
A program may use at most 64 MiB of HBM per device.

v0:
```python
import math
import jax
import jax.numpy as jnp
from jax import lax
from jax.sharding import PartitionSpec as P


def sketch_rows(rows_x, rows_y, weight_part):
    count_exp = weight_part.shape[0]
    row_count = rows_x.shape[0]
    sketch_rank = rows_y.shape[1]
    rows_wide = rows_y.astype(jnp.float32)
    contract = (((0,), (0,)), ((), ()))
    scaled = (weight_part.T[:, :, None] * rows_wide[:, None, :]).astype(jnp.bfloat16)
    scaled = scaled.reshape(row_count, count_exp * sketch_rank)
    return lax.dot_general(rows_x, scaled, contract, preferred_element_type=jnp.float32)


def gram_of(sketch_flat, sketch_rank):
    shaped = sketch_flat.reshape(sketch_flat.shape[0], -1, sketch_rank)
    return jnp.einsum("dkr,dks->rs", shaped, shaped, precision=lax.Precision.HIGHEST)


def on_device(activations, out_grads, sketch_op, block_lists, block_counts, gate_values):
    sketch_rank = sketch_op.shape[1]
    feat_width = activations.shape[1]
    local_exp = block_lists.shape[0]
    blocks = block_lists.shape[1]
    partial_sketch = jnp.dot(out_grads, sketch_op, preferred_element_type=jnp.float32)
    sketched = lax.psum(partial_sketch, "group").astype(jnp.bfloat16)
    slot_ids = jnp.arange(blocks, dtype=jnp.int32)
    slot_live = slot_ids[None, :] < block_counts[:, None]
    onehot = ((block_lists[:, :, None] == slot_ids[None, None, :]) & slot_live[:, :, None]).astype(
        jnp.float32
    )
    weights = jnp.einsum("ejb,ejt->ebt", onehot, gate_values.astype(jnp.float32)).reshape(
        local_exp, -1
    )
    piece_rows = lax.all_gather(activations, "expert", axis=0, tiled=True)
    piece_sketch = lax.all_gather(sketched, "expert", axis=0, tiled=True)
    sketch_all = sketch_rows(piece_rows, piece_sketch, weights)
    gram_total = lax.psum(gram_of(sketch_all, sketch_rank), ("expert", "group"))
    factor = jnp.linalg.cholesky(gram_total)
    stacked = (
        sketch_all.reshape(feat_width, local_exp, sketch_rank)
        .transpose(1, 0, 2)
        .reshape(-1, sketch_rank)
    )
    basis_flat = lax.linalg.triangular_solve(
        factor, stacked, left_side=False, lower=True, transpose_a=True
    )
    out_scale = math.sqrt(local_exp * lax.axis_size("expert") * feat_width * lax.axis_size("group"))
    return (basis_flat * out_scale).reshape(local_exp, feat_width, sketch_rank)


def solution(mesh):
    in_specs = (
        P("expert", "group"),
        P("expert", "group"),
        P("group", None),
        P("expert", None),
        P("expert"),
        P("expert", None, None),
    )
    out_specs = P("expert", "group", None)
    return jax.shard_map(
        on_device, mesh=mesh, in_specs=in_specs, out_specs=out_specs, check_vma=False
    )
```

profile of v0, /device:TPU:1, one launch (start us, length us, event | category | flops | bytes accessed | tf_op | source)
XLA Modules:
  0.0 443.5 jit_solution(5734964180359648877)
XLA Ops:
  6.5 0.0 copy-start
  6.5 0.0 all-gather.3.cloned.1.call-start
  6.5 0.9 copy-done
  7.5 1.1 fusion.10
  8.6 27.5 %psum.14 = bf16[128,128]{1,0:T(8,128)(2,1)} all-reduce(f32[128,128]{1,0:T(8,128)S(1)} %fusion.10), channel_id=1, replica_groups=mesh['expert'=32,'group'=8] {'group'}, use_global_device_ids=true, to_apply=%region_0.0 | all-reduce | flops 16384 | bytes 98304 | tf_op jit(solution)/shard_map/psum | solution.py:30
  36.2 0.0 all-gather.3.cloned.1.call-update
  36.2 0.0 all-gather.5.cloned.1.call-start
  36.2 0.7 all-gather.5.cloned.1.call-update
  36.9 0.0 all-reduce.2.cloned.1.call-start
  37.0 0.7 iota_compare_fusion.3
  37.7 1.0 convolution_bitcast_fusion
  38.7 0.1 copy.26
  38.8 0.6 copy.11
  39.4 50.1 %all-gather.3.cloned.1.call-done = bf16[4096,128]{1,0:T(8,128)(2,1)} async-done(((bf16[128,128]{1,0:T(8,128)(2,1)}), bf16[4096,128]{1,0:T(8,128)(2,1)}) %all-gather.3.cloned.1.call-update) | async-done | bytes 1048592 | tf_op jit(solution)/shard_map/all_gather | solution.py:40
  89.5 1.4 convert_element_type.16
  90.9 16.4 %multiply_convert_fusion = bf16[4096,8,128]{2,1,0:T(8,128)(2,1)} fusion(f32[4096,128]{1,0:T(8,128)S(1)} %convert_element_type.16, f32[4096,8]{1,0:T(8,128)S(1)} %copy.11), kind=kLoop, calls=%fused_computation | loop fusion | flops 8388608 | bytes 10616832 | tf_op jit(solution)/shard_map/convert_element_type | solution.py:14
  107.2 40.0 %all-gather.5.cloned.1.call-done = bf16[4096,896]{1,0:T(8,128)(2,1)} async-done(((bf16[128,896]{1,0:T(8,128)(2,1)}), bf16[4096,896]{1,0:T(8,128)(2,1)}) %all-gather.5.cloned.1.call-update) | async-done | bytes 7340048 | tf_op jit(solution)/shard_map/all_gather | solution.py:39
  147.3 12.9 %fusion = f32[1024,896]{1,0:T(8,128)S(1)} fusion(bf16[4096,896]{1,0:T(8,128)(2,1)} %all-gather.5.cloned.1.call-done, bf16[512,8,8,128]{3,2,1,0:T(8,128)(2,1)} %bitcast.40), kind=kOutput, calls=%fused_computation.2 | convolution fusion | flops 7516192768 | bytes 19398656 | tf_op jit(solution)/shard_map/dot_general | solution.py:16
  160.2 0.0 copy-start.1
  160.2 1.8 copy-done.1
  162.1 3.6 convolution_bitcast_fusion.1
  165.7 0.0 all-reduce.2.cloned.1.call-update
  165.7 5.0 %copy.12 = f32[896,8,128]{2,0,1:T(8,128)} copy(f32[896,8,128]{0,2,1:T(8,128)} %bitcast.38) | data formatting | bytes 7340032 | tf_op jit(solution)/shard_map/reshape | solution.py:45
  170.7 235.7 %all-reduce.2.cloned.1.call-done = f32[128,128]{0,1:T(8,128)} async-done(((f32[128,128]{0,1:T(8,128)}), f32[128,128]{0,1:T(8,128)}) %all-reduce.2.cloned.1.call-update) | async-done | bytes 65552 | tf_op jit(solution)/shard_map/psum | solution.py:42
  406.4 0.9 copy.15
  407.4 0.9 fusion.7
  408.2 11.7 %cholesky.16 = f32[128,128]{1,0:T(8,128)S(1)} custom-call(f32[128,128]{1,0:T(8,128)S(1)} %fusion.7), custom_call_target="Cholesky" | custom-call | tf_op jit(solution)/shard_map/jit(cholesky)/cholesky | solution.py:43
  420.0 0.6 compare_reduce_fusion
  420.6 0.7 fusion.5
  421.3 9.8 %custom-call.6 = f32[1,128,128]{1,2,0:T(8,128)S(1)} custom-call(f32[1,128,128]{2,1,0:T(8,128)S(1)} %fusion.5), custom_call_target="InvertDiagBlocksLowerTriangular" | custom-call | tf_op jit(solution)/shard_map/triangular_solve | solution.py:49
  431.1 5.9 %convolution_multiply_fusion = f32[7168,128]{1,0:T(8,128)} fusion(f32[7168,128]{1,0:T(8,128)} %bitcast.39, f32[1,128,128]{1,2,0:T(8,128)S(1)} %custom-call.6), kind=kOutput, calls=%fused_computation.1 | convolution fusion | flops 1410203648 | bytes 7405568 | tf_op jit(solution)/shard_map/triangular_solve | solution.py:49
  (1 shorter events, 0.0 us)
Async XLA Ops:
  6.5 0.9 copy-start
  6.5 83.0 %all-gather.3.cloned.1.call-start = ((), (), s32[]{:S(2)}) async-start(), calls=%async_computation | async-start | bytes 1081344 | tf_op jit(solution)/shard_map/all_gather | solution.py:40
  36.2 111.1 %all-gather.5.cloned.1.call-start = ((), (), s32[]{:S(2)}) async-start(), calls=%async_computation.1 | async-start | bytes 7569408 | tf_op jit(solution)/shard_map/all_gather | solution.py:39
  36.9 369.5 %all-reduce.2.cloned.1.call-start = ((), (), s32[]{:S(2)}) async-start(), calls=%async_computation.2 | async-start | bytes 131072 | tf_op jit(solution)/shard_map/psum | solution.py:42
  160.2 1.8 copy-start.1
Sparse Core Ops, SparseCore 0:
  36.3 53.1 all-gather.2
  92.0 55.1 all-gather.4
  165.8 240.5 all-reduce.1
where the time goes:
time: 444 us
  waiting for transfers between devices  327 us (74%)
  other arithmetic  42.2 us (10%)
  blocking collectives  27.5 us (6%)
  matrix products  24.7 us (6%)
  between operations  13.2 us (3%)
  local copies, waits for them, and re-layouts  9.39 us (2%)
    psum x1, waiting for transfers between devices, on_device(): gram_total = lax.psum(gram_of(sketch_all, sketch_rank), ('expert', 'group'))  236 us
    all_gather x1, waiting for transfers between devices, on_device(): piece_sketch = lax.all_gather(sketched, 'expert', axis=0, tiled=True)  50.1 us
    all_gather x1, waiting for transfers between devices, on_device(): piece_rows = lax.all_gather(activations, 'expert', axis=0, tiled=True)  40 us
    psum x1, blocking collectives, on_device(): sketched = lax.psum(partial_sketch, 'group').astype(jnp.bfloat16)  27.5 us
    convert_element_type x1, other arithmetic, sketch_rows(): (weight_part.T[:, :, None] * rows_wide[:, None, :]).astype(jnp.bfloat16)  16.4 us
    dot_general x1, matrix products, sketch_rows(): lax.dot_general(rows_x, scaled, contract, preferred_element_type=jnp.floa...  12.9 us
    another operation x3, other arithmetic, on_device(): factor = jnp.linalg.cholesky(gram_total)  12.4 us
    another operation x2, other arithmetic, on_device(): lax.linalg.triangular_solve(factor, stacked, left_side=False, lower=True,...  10.5 us
  transfers between devices with their start and end apart: 3, of which 3 were waited for; matrix products, arithmetic and copies ran while one was open for 6% of the time, Pallas kernels for 0%

commit v1 on v0

--- a/solution.py
+++ b/solution.py
@@ -39,7 +39,10 @@
     piece_rows = lax.all_gather(activations, "expert", axis=0, tiled=True)
     piece_sketch = lax.all_gather(sketched, "expert", axis=0, tiled=True)
     sketch_all = sketch_rows(piece_rows, piece_sketch, weights)
-    gram_total = lax.psum(gram_of(sketch_all, sketch_rank), ("expert", "group"))
+    ticks_feed = lambda local_block, axis_tag, peer_axis: jax.lax.psum(
+        jax.lax.psum(local_block, axis_tag), axis_name=peer_axis
+    )
+    gram_total = ticks_feed(gram_of(sketch_all, sketch_rank), "expert", "group")
     factor = jnp.linalg.cholesky(gram_total)
     stacked = (
         sketch_all.reshape(feat_width, local_exp, sketch_rank)

time: 444 us -> 382 us (0.86)
  waiting for transfers between devices: 327 us -> 260 us
    psum x1 -> x2, waiting for transfers between devices: 236 us -> 170 us  [the longest x1 106 us: on_device(): jax.lax.psum(local_block, axis_tag)]
  transfers between devices with their start and end apart: 3 -> 4, of which waited for: 3 -> 4; matrix products, arithmetic and copies ran while one was open for 6% -> 7% of each run, Pallas kernels for 0% -> 0%
where the time goes in v1:
time: 382 us; the launch traced here: 378 us
  waiting for transfers between devices  260 us (68%)
  other arithmetic  42.2 us (11%)
  blocking collectives  27.5 us (7%)
  matrix products  24.7 us (6%)
  between operations  13.2 us (3%)
  local copies, waits for them, and re-layouts  9.39 us (2%)
    psum x1, waiting for transfers between devices, on_device(): jax.lax.psum(local_block, axis_tag)  106 us
    psum x1, waiting for transfers between devices, on_device(): jax.lax.psum(jax.lax.psum(local_block, axis_tag), axis_name=peer_axis)  63.2 us
    all_gather x1, waiting for transfers between devices, on_device(): piece_sketch = lax.all_gather(sketched, 'expert', axis=0, tiled=True)  50.1 us
    all_gather x1, waiting for transfers between devices, on_device(): piece_rows = lax.all_gather(activations, 'expert', axis=0, tiled=True)  40 us
    psum x1, blocking collectives, on_device(): sketched = lax.psum(partial_sketch, 'group').astype(jnp.bfloat16)  27.5 us
    convert_element_type x1, other arithmetic, sketch_rows(): (weight_part.T[:, :, None] * rows_wide[:, None, :]).astype(jnp.bfloat16)  16.4 us
    dot_general x1, matrix products, sketch_rows(): lax.dot_general(rows_x, scaled, contract, preferred_element_type=jnp.floa...  12.9 us
    another operation x3, other arithmetic, on_device(): factor = jnp.linalg.cholesky(gram_total)  12.4 us
  transfers between devices with their start and end apart: 4, of which 4 were waited for; matrix products, arithmetic and copies ran while one was open for 7% of the time, Pallas kernels for 0%

profile of v1, /device:TPU:1, one launch (start us, length us, event | category | flops | bytes accessed | tf_op | source)
XLA Modules:
  0.0 377.7 jit_solution(11500558794340875962)
XLA Ops:
  6.5 0.0 copy-start
  6.5 0.0 all-gather.3.cloned.1.call-start
  6.5 0.9 copy-done
  7.5 1.1 fusion.10
  8.6 27.5 %psum.21 = bf16[128,128]{1,0:T(8,128)(2,1)} all-reduce(f32[128,128]{1,0:T(8,128)S(1)} %fusion.10), channel_id=1, replica_groups=mesh['expert'=32,'group'=8] {'group'}, use_global_device_ids=true, to_apply=%region_0.0 | all-reduce | flops 16384 | bytes 98304 | tf_op jit(solution)/shard_map/psum | solution.py:30
  36.2 0.0 all-gather.3.cloned.1.call-update
  36.2 0.0 all-gather.5.cloned.1.call-start
  36.2 0.7 all-gather.5.cloned.1.call-update
  36.9 0.0 all-reduce.3.cloned.1.call-start
  37.0 0.7 iota_compare_fusion.3
  37.7 1.0 convolution_bitcast_fusion
  38.7 0.1 copy.26
  38.8 0.6 copy.11
  39.4 50.1 %all-gather.3.cloned.1.call-done = bf16[4096,128]{1,0:T(8,128)(2,1)} async-done(((bf16[128,128]{1,0:T(8,128)(2,1)}), bf16[4096,128]{1,0:T(8,128)(2,1)}) %all-gather.3.cloned.1.call-update) | async-done | bytes 1048592 | tf_op jit(solution)/shard_map/all_gather | solution.py:40
  89.5 1.4 convert_element_type.16
  90.9 16.4 %multiply_convert_fusion = bf16[4096,8,128]{2,1,0:T(8,128)(2,1)} fusion(f32[4096,128]{1,0:T(8,128)S(1)} %convert_element_type.16, f32[4096,8]{1,0:T(8,128)S(1)} %copy.11), kind=kLoop, calls=%fused_computation | loop fusion | flops 8388608 | bytes 10616832 | tf_op jit(solution)/shard_map/convert_element_type | solution.py:14
  107.2 40.0 %all-gather.5.cloned.1.call-done = bf16[4096,896]{1,0:T(8,128)(2,1)} async-done(((bf16[128,896]{1,0:T(8,128)(2,1)}), bf16[4096,896]{1,0:T(8,128)(2,1)}) %all-gather.5.cloned.1.call-update) | async-done | bytes 7340048 | tf_op jit(solution)/shard_map/all_gather | solution.py:39
  147.3 12.9 %fusion = f32[1024,896]{1,0:T(8,128)S(1)} fusion(bf16[4096,896]{1,0:T(8,128)(2,1)} %all-gather.5.cloned.1.call-done, bf16[512,8,8,128]{3,2,1,0:T(8,128)(2,1)} %bitcast.40), kind=kOutput, calls=%fused_computation.2 | convolution fusion | flops 7516192768 | bytes 19398656 | tf_op jit(solution)/shard_map/dot_general | solution.py:16
  160.2 0.0 copy-start.1
  160.2 1.8 copy-done.1
  162.1 3.6 convolution_bitcast_fusion.1
  165.7 0.0 all-reduce.3.cloned.1.call-update
  165.7 0.2 all-reduce.5.cloned.1.call-start
  166.0 106.4 %all-reduce.3.cloned.1.call-done = f32[128,128]{0,1:T(8,128)} async-done(((f32[128,128]{0,1:T(8,128)}), f32[128,128]{0,1:T(8,128)}) %all-reduce.3.cloned.1.call-update) | async-done | bytes 65552 | tf_op jit(solution)/shard_map/psum | solution.py:43
  272.3 0.0 all-reduce.5.cloned.1.call-update
  272.4 5.0 %copy.12 = f32[896,8,128]{2,0,1:T(8,128)} copy(f32[896,8,128]{0,2,1:T(8,128)} %bitcast.38) | data formatting | bytes 7340032 | tf_op jit(solution)/shard_map/reshape | solution.py:48
  277.4 63.2 %all-reduce.5.cloned.1.call-done = f32[128,128]{0,1:T(8,128)} async-done(((f32[128,128]{0,1:T(8,128)}), f32[128,128]{0,1:T(8,128)}) %all-reduce.5.cloned.1.call-update) | async-done | bytes 65552 | tf_op jit(solution)/shard_map/psum | solution.py:42
  340.6 0.9 copy.15
  341.5 0.9 fusion.7
  342.3 11.7 %cholesky.16 = f32[128,128]{1,0:T(8,128)S(1)} custom-call(f32[128,128]{1,0:T(8,128)S(1)} %fusion.7), custom_call_target="Cholesky" | custom-call | tf_op jit(solution)/shard_map/jit(cholesky)/cholesky | solution.py:46
  354.1 0.6 compare_reduce_fusion
  354.7 0.7 fusion.5
  355.4 9.8 %custom-call.6 = f32[1,128,128]{1,2,0:T(8,128)S(1)} custom-call(f32[1,128,128]{2,1,0:T(8,128)S(1)} %fusion.5), custom_call_target="InvertDiagBlocksLowerTriangular" | custom-call | tf_op jit(solution)/shard_map/triangular_solve | solution.py:52
  365.2 5.9 %convolution_multiply_fusion = f32[7168,128]{1,0:T(8,128)} fusion(f32[7168,128]{1,0:T(8,128)} %bitcast.39, f32[1,128,128]{1,2,0:T(8,128)S(1)} %custom-call.6), kind=kOutput, calls=%fused_computation.1 | convolution fusion | flops 1410203648 | bytes 7405568 | tf_op jit(solution)/shard_map/triangular_solve | solution.py:52
  (1 shorter events, 0.0 us)
Async XLA Ops:
  6.5 0.9 copy-start
  6.5 83.0 %all-gather.3.cloned.1.call-start = ((), (), s32[]{:S(2)}) async-start(), calls=%async_computation | async-start | bytes 1081344 | tf_op jit(solution)/shard_map/all_gather | solution.py:40
  36.2 111.1 %all-gather.5.cloned.1.call-start = ((), (), s32[]{:S(2)}) async-start(), calls=%async_computation.1 | async-start | bytes 7569408 | tf_op jit(solution)/shard_map/all_gather | solution.py:39
  36.9 235.4 %all-reduce.3.cloned.1.call-start = ((), (), s32[]{:S(2)}) async-start(), calls=%async_computation.2 | async-start | bytes 131072 | tf_op jit(solution)/shard_map/psum | solution.py:43
  160.2 1.8 copy-start.1
  165.7 174.8 %all-reduce.5.cloned.1.call-start = ((), (), s32[]{:S(2)}) async-start(), calls=%async_computation.3 | async-start | bytes 131072 | tf_op jit(solution)/shard_map/psum | solution.py:42
Sparse Core Ops, SparseCore 0:
  36.3 53.1 all-gather.2
  92.0 55.1 all-gather.4
  165.8 106.4 all-reduce.2
  274.5 66.0 all-reduce.4
